TPU v7x, 512 devices: a whole 4x4x16 slice. The times are simulated.
512 devices in a mesh: lat: 16 (over x_lo, y, core), lon: 32 (over x_hi, z).
Axes of the slice: x: 4 (x_hi: 2, x_lo: 2; x = x_hi * 2 + x_lo), y: 4, z: 16, core: 2. Of those that a mesh axis runs over, the one named last changes fastest.
Arguments:
- field: float32 [256, 16, 4096], P(None, 'lat', 'lon'), may hold values from -6 to 6
- cotangent: float32 [256, 16, 4096], P(None, 'lat', 'lon'), may hold values from -6 to 6
- conv_weight: float32 [3, 3, 256, 256], replicated, may hold values from -0.125 to 0.125
- spectral_filter: float32 [2, 256, 4096], P(None, None, 'lon'), may hold values from -6 to 6
Outputs:
- output: float32 [256, 16, 4096], P(None, 'lat', 'lon')
- input_grad: float32 [256, 16, 4096], P(None, 'lat', 'lon')
- filter_grad: float32 [2, 256, 4096], P(None, None, 'lon')
All inputs are finite; a program needn't handle non-finite values.
Results may differ from a plain program's by a relative error of at most 0.00014.
Values sent between devices are 32-bit elements; how exact they have to be, the bound alone decides.
A program may use at most 64 MiB of HBM per device.

v0:
```python
import jax
import jax.numpy as jnp
from jax import lax
from jax.sharding import PartitionSpec as P

precise = lax.Precision.HIGHEST


def padded_2(array, sides, width, wrap):
    for axis, dim in sides:
        peers, length = (lax.axis_size(axis), array.shape[dim])
        up = [(i, (i + 1) % peers) for i in range(peers if wrap else peers - 1)]
        down = [(j, i) for i, j in up]
        last = lax.slice_in_dim(array, length - width, length, axis=dim)
        leading = lax.slice_in_dim(array, 0, width, axis=dim)
        before = lax.ppermute(last, axis, up)
        after = lax.ppermute(leading, axis, down)
        array = jnp.concatenate([before, array, after], axis=dim)
    return array


def partner(array, axis, stride):
    return lax.ppermute(array, axis, [(i, i ^ 1 << stride) for i in range(lax.axis_size(axis))])


def angle_table(first, second, modulus):
    product = first[:, None] * second[None, :] % modulus
    return 2.0 * jnp.pi / modulus * product.astype(jnp.float32)


def apply_taps(padded, taps, lat_rows, columns):
    total = jnp.zeros((taps.shape[2], lat_rows, columns), jnp.float32)
    for tap_row in range(3):
        for tap_col in range(3):
            window = padded[:, tap_row : tap_row + lat_rows, tap_col : tap_col + columns]
            total = total + jnp.einsum(
                "oi,iab->oab", taps[tap_row, tap_col], window, precision=precise
            )
    return total


def with_rims(field):
    wider = padded_2(field, (("lon", 2),), 1, True)
    return padded_2(wider, (("lat", 1),), 1, False)


def local_forward(real_part, imag_part):
    columns = real_part.shape[-1]
    places = lax.iota(jnp.int32, columns)
    angles = angle_table(places, places, columns)
    cosine = jnp.cos(angles)
    sine = jnp.sin(angles)
    out_real = jnp.dot(real_part, cosine, precision=precise) + jnp.dot(
        imag_part, sine, precision=precise
    )
    out_imag = jnp.dot(imag_part, cosine, precision=precise) - jnp.dot(
        real_part, sine, precision=precise
    )
    return (out_real, out_imag)


def local_inverse(real_part, imag_part):
    columns = real_part.shape[-1]
    places = lax.iota(jnp.int32, columns)
    angles = angle_table(places, places, columns)
    cosine = jnp.cos(angles)
    sine = jnp.sin(angles)
    out_real = jnp.dot(real_part, cosine, precision=precise) - jnp.dot(
        imag_part, sine, precision=precise
    )
    out_imag = jnp.dot(imag_part, cosine, precision=precise) + jnp.dot(
        real_part, sine, precision=precise
    )
    return (out_real / columns, out_imag / columns)


def section_angles(place, bit_pos, columns):
    offsets = lax.iota(jnp.int32, columns)
    start = place % 2**bit_pos * columns
    span = 2 * columns * 2**bit_pos
    angles = 2.0 * jnp.pi / span * (start + offsets).astype(jnp.float32)
    upper = place // 2**bit_pos % 2 == 1
    return (jnp.cos(angles), jnp.sin(angles), upper)


def forward_pairs(field):
    extent = lax.axis_size("lon")
    width_bits = extent.bit_length() - 1
    place = lax.axis_index("lon")
    columns = field.shape[-1]
    data = jnp.stack([field, jnp.zeros_like(field)])
    for bit_pos in reversed(range(width_bits)):
        other = partner(data, "lon", bit_pos)
        cosine, sine, upper = section_angles(place, bit_pos, columns)
        differ = other - data
        turned = jnp.stack(
            [differ[0] * cosine + differ[1] * sine, differ[1] * cosine - differ[0] * sine]
        )
        data = jnp.where(upper, turned, data + other)
    out_real, out_imag = local_forward(data[0], data[1])
    return jnp.stack([out_real, out_imag])


def inverse_pairs(spectrum):
    extent = lax.axis_size("lon")
    width_bits = extent.bit_length() - 1
    place = lax.axis_index("lon")
    columns = spectrum.shape[-1]
    back_real, back_imag = local_inverse(spectrum[0], spectrum[1])
    data = jnp.stack([back_real, back_imag])
    for bit_pos in range(width_bits):
        cosine, sine, upper = section_angles(place, bit_pos, columns)
        turned = jnp.stack([data[0] * cosine - data[1] * sine, data[1] * cosine + data[0] * sine])
        outgoing = jnp.where(upper, turned, data)
        other = partner(outgoing, "lon", bit_pos)
        data = jnp.where(upper, other - outgoing, outgoing + other) * 0.5
    return data[0]


def on_device(field, cotangent, conv_weight, spectral_filter):
    lat_rows = field.shape[1]
    columns = field.shape[2]
    total_len = columns * lax.axis_size("lon")
    mixed = apply_taps(with_rims(field), conv_weight, lat_rows, columns)
    hidden_spec = forward_pairs(mixed)
    cot_spec = forward_pairs(cotangent)
    gain_real = spectral_filter[0][:, None, :]
    gain_imag = spectral_filter[1][:, None, :]
    filtered = jnp.stack(
        [
            gain_real * hidden_spec[0] - gain_imag * hidden_spec[1],
            gain_real * hidden_spec[1] + gain_imag * hidden_spec[0],
        ]
    )
    adjoint = jnp.stack(
        [
            gain_real * cot_spec[0] + gain_imag * cot_spec[1],
            gain_real * cot_spec[1] - gain_imag * cot_spec[0],
        ]
    )
    shaped = inverse_pairs(filtered)
    back_field = inverse_pairs(adjoint)
    output = field + shaped
    local_grad = (
        jnp.stack(
            [
                jnp.sum(hidden_spec[0] * cot_spec[0] + hidden_spec[1] * cot_spec[1], axis=1),
                jnp.sum(hidden_spec[0] * cot_spec[1] - hidden_spec[1] * cot_spec[0], axis=1),
            ]
        )
        / total_len
    )
    filter_grad = lax.psum(local_grad, "lat")
    flipped_taps = jnp.transpose(conv_weight[::-1, ::-1], (0, 1, 3, 2))
    input_grad = cotangent + apply_taps(with_rims(back_field), flipped_taps, lat_rows, columns)
    return (output, input_grad, filter_grad)


def solution(mesh):
    placed = (P(None, "lat", "lon"), P(None, "lat", "lon"), P(), P(None, None, "lon"))
    return jax.shard_map(
        on_device,
        mesh=mesh,
        in_specs=placed,
        out_specs=(P(None, "lat", "lon"), P(None, "lat", "lon"), P(None, None, "lon")),
        check_vma=False,
    )
```

profile of v0, /device:TPU:1, one launch (start us, length us, event | category | flops | bytes accessed | tf_op | source)
XLA Modules:
  0.0 503.1 jit_solution(4956193246249797645)
XLA Ops:
  8.7 4.4 collective-permute-start
  13.1 12.0 %collective-permute-start.1 = (f32[256,1,1]{2,1,0:T(1,128)S(1)}, f32[256,1,1]{2,1,0:T(1,128)S(1)}, u32[]{:S(2)}, u32[]{:S(2)}) collective-permute-start(f32[256,1,1]{2,1,0:T(1,128)S(1)} %get-tuple-element.71), channel_id=1, source_target_pairs={{1,0},{2,1},{3,2},{4,3},{5,4},{6,5},{7,6},{8,7},{9,8},{10,9},{11,1... | collective-permute-start | bytes 3080 | tf_op jit(solution)/shard_map/ppermute | solution.py:17
  26.1 2.1 collective-permute-start.14
  30.0 3.1 collective-permute-start.3
  33.2 3.1 collective-permute-start.2
  36.3 1.9 pad_maximum_fusion.4
  43.8 4.6 collective-permute-start.4
  48.6 6.7 %collective-permute-done.4 = f32[2,256,1,128]{1,3,2,0:T(8,128)S(1)} collective-permute-done((f32[2,256,1,128]{1,3,2,0:T(8,128)}, f32[2,256,1,128]{1,3,2,0:T(8,128)S(1)}, u32[]{:S(2)}, u32[]{:S(2)}) %collective-permute-start.4) | collective-permute-done | bytes 262176 | tf_op jit(solution)/shard_map/ppermute | solution.py:23
  56.4 9.2 %collective-permute-start.5 = (f32[2,256,1,128]{1,3,2,0:T(8,128)}, f32[2,256,1,128]{1,3,2,0:T(8,128)}, u32[]{:S(2)}, u32[]{:S(2)}) collective-permute-start(f32[2,256,1,128]{1,3,2,0:T(8,128)} %maximum_select_fusion), channel_id=1, source_target_pairs={{0,8},{1,9},{2,10},{3,11},{4,12},{5,13},{6,14},{7,15},{8,0},{9,1},... | collective-permute-start | bytes 786440 | tf_op jit(solution)/shard_map/ppermute | solution.py:23
  66.4 4.8 collective-permute-start.15
  71.2 20.3 %collective-permute-done.5 = f32[2,256,1,128]{1,3,2,0:T(8,128)} collective-permute-done((f32[2,256,1,128]{1,3,2,0:T(8,128)}, f32[2,256,1,128]{1,3,2,0:T(8,128)}, u32[]{:S(2)}, u32[]{:S(2)}) %collective-permute-start.5) | collective-permute-done | bytes 262176 | tf_op jit(solution)/shard_map/ppermute | solution.py:23
  92.5 20.8 %collective-permute-done.15 = f32[2,256,1,128]{1,3,2,0:T(8,128)} collective-permute-done((f32[2,256,1,128]{1,3,2,0:T(8,128)}, f32[2,256,1,128]{1,3,2,0:T(8,128)}, u32[]{:S(2)}, u32[]{:S(2)}) %collective-permute-start.15) | collective-permute-done | bytes 262176 | tf_op jit(solution)/shard_map/ppermute | solution.py:23
  115.6 1.9 collective-permute-start.16
  118.7 7.3 %collective-permute-start.6 = (f32[2,256,1,128]{1,3,2,0:T(8,128)S(1)}, f32[2,256,1,128]{1,3,2,0:T(8,128)}, u32[]{:S(2)}, u32[]{:S(2)}) collective-permute-start(f32[2,256,1,128]{1,3,2,0:T(8,128)S(1)} %maximum_select_fusion.1), channel_id=1, source_target_pairs={{0,4},{1,5},{2,6},{3,7},{4,0},{5,1},{6,2},{7,3},{8,12},{9,13},{10,... | collective-permute-start | bytes 786440 | tf_op jit(solution)/shard_map/ppermute | solution.py:23
  126.1 30.2 %collective-permute-done.16 = f32[2,256,1,128]{1,3,2,0:T(8,128)} collective-permute-done((f32[2,256,1,128]{1,3,2,0:T(8,128)S(1)}, f32[2,256,1,128]{1,3,2,0:T(8,128)}, u32[]{:S(2)}, u32[]{:S(2)}) %collective-permute-start.16) | collective-permute-done | bytes 262176 | tf_op jit(solution)/shard_map/ppermute | solution.py:23
  157.3 4.6 collective-permute-done.6
  164.0 1.9 collective-permute-start.17
  167.0 4.3 collective-permute-start.7
  171.3 10.2 %collective-permute-done.17 = f32[2,256,1,128]{1,3,2,0:T(8,128)} collective-permute-done((f32[2,256,1,128]{1,3,2,0:T(8,128)S(1)}, f32[2,256,1,128]{1,3,2,0:T(8,128)}, u32[]{:S(2)}, u32[]{:S(2)}) %collective-permute-start.17) | collective-permute-done | bytes 262176 | tf_op jit(solution)/shard_map/ppermute | solution.py:23
  182.5 4.6 collective-permute-done.7
  189.3 1.9 collective-permute-start.18
  192.2 3.5 collective-permute-start.8
  195.9 2.8 collective-permute-done.18
  199.6 4.5 collective-permute-done.8
  215.2 2.2 collective-permute-start.19
  217.5 3.0 collective-permute-start.9
  220.6 3.0 collective-permute-done.19
  223.6 5.6 %collective-permute-done.9 = f32[2,256,1,128]{1,3,2,0:T(8,128)S(1)} collective-permute-done((f32[2,256,1,128]{1,3,2,0:T(8,128)S(1)}, f32[2,256,1,128]{1,3,2,0:T(8,128)S(1)}, u32[]{:S(2)}, u32[]{:S(2)}) %collective-permute-start.9) | collective-permute-done | bytes 262176 | tf_op jit(solution)/shard_map/ppermute | solution.py:23
  229.5 1.9 collective-permute-start.10
  231.5 4.3 collective-permute-start.20
  235.7 15.6 %collective-permute-done.10 = f32[2,256,1,128]{1,3,2,0:T(8,128)S(1)} collective-permute-done((f32[2,256,1,128]{1,3,2,0:T(8,128)S(1)}, f32[2,256,1,128]{1,3,2,0:T(8,128)S(1)}, u32[]{:S(2)}, u32[]{:S(2)}) %collective-permute-start.10) | collective-permute-done | bytes 262176 | tf_op jit(solution)/shard_map/ppermute | solution.py:23
  251.4 5.6 %collective-permute-done.20 = f32[2,256,1,128]{1,3,2,0:T(8,128)S(1)} collective-permute-done((f32[2,256,1,128]{1,3,2,0:T(8,128)S(1)}, f32[2,256,1,128]{1,3,2,0:T(8,128)S(1)}, u32[]{:S(2)}, u32[]{:S(2)}) %collective-permute-start.20) | collective-permute-done | bytes 262176 | tf_op jit(solution)/shard_map/ppermute | solution.py:23
  257.2 3.8 collective-permute-start.11
  261.1 5.4 %collective-permute-start.21 = (f32[2,256,1,128]{1,3,2,0:T(8,128)S(1)}, f32[2,256,1,128]{1,3,2,0:T(8,128)S(1)}, u32[]{:S(2)}, u32[]{:S(2)}) collective-permute-start(f32[2,256,1,128]{1,3,2,0:T(8,128)S(1)} %maximum_select_fusion.17), channel_id=1, source_target_pairs={{0,4},{1,5},{2,6},{3,7},{4,0},{5,1},{6,2},{7,3},{8,12},{9,13},{10,... | collective-permute-start | bytes 786440 | tf_op jit(solution)/shard_map/ppermute | solution.py:23
  266.4 35.6 %collective-permute-done.11 = f32[2,256,1,128]{1,3,2,0:T(8,128)S(1)} collective-permute-done((f32[2,256,1,128]{1,3,2,0:T(8,128)S(1)}, f32[2,256,1,128]{1,3,2,0:T(8,128)S(1)}, u32[]{:S(2)}, u32[]{:S(2)}) %collective-permute-start.11) | collective-permute-done | bytes 262176 | tf_op jit(solution)/shard_map/ppermute | solution.py:23
  302.1 16.9 %collective-permute-done.21 = f32[2,256,1,128]{1,3,2,0:T(8,128)S(1)} collective-permute-done((f32[2,256,1,128]{1,3,2,0:T(8,128)S(1)}, f32[2,256,1,128]{1,3,2,0:T(8,128)S(1)}, u32[]{:S(2)}, u32[]{:S(2)}) %collective-permute-start.21) | collective-permute-done | bytes 262176 | tf_op jit(solution)/shard_map/ppermute | solution.py:23
  320.6 10.3 %collective-permute-start.12 = (f32[2,256,1,128]{1,3,2,0:T(8,128)}, f32[2,256,1,128]{1,3,2,0:T(8,128)}, u32[]{:S(2)}, u32[]{:S(2)}) collective-permute-start(f32[2,256,1,128]{1,3,2,0:T(8,128)} %maximum_select_fusion.8), channel_id=1, source_target_pairs={{0,8},{1,9},{2,10},{3,11},{4,12},{5,13},{6,14},{7,15},{8,0},{9,1},... | collective-permute-start | bytes 786440 | tf_op jit(solution)/shard_map/ppermute | solution.py:23
  331.6 3.7 collective-permute-start.22
  337.7 4.7 collective-permute-done.12
  343.6 6.0 %collective-permute-done.22 = f32[2,256,1,128]{1,3,2,0:T(8,128)} collective-permute-done((f32[2,256,1,128]{1,3,2,0:T(8,128)}, f32[2,256,1,128]{1,3,2,0:T(8,128)}, u32[]{:S(2)}, u32[]{:S(2)}) %collective-permute-start.22) | collective-permute-done | bytes 262176 | tf_op jit(solution)/shard_map/ppermute | solution.py:23
  350.8 1.9 collective-permute-start.23
  353.5 4.9 collective-permute-start.13
  358.4 1.9 collective-permute-done.23
  361.2 1.9 collective-permute-start.24
  363.1 8.9 %collective-permute-start.25 = (f32[256,1,1]{0,2,1:T(1,128)S(1)}, f32[256,1,1]{0,2,1:T(1,128)S(1)}, u32[]{:S(2)}, u32[]{:S(2)}) collective-permute-start(f32[256,1,1]{0,2,1:T(1,128)S(1)} %get-tuple-element.63), channel_id=1, source_target_pairs={{1,0},{2,1},{3,2},{4,3},{5,4},{6,5},{7,6},{8,7},{9,8},{10,9},{11,1... | collective-permute-start | bytes 3080 | tf_op jit(solution)/shard_map/ppermute | solution.py:17
  374.0 5.7 %collective-permute-start.27 = (f32[256,1,130]{0,2,1:T(8,128)S(1)}, f32[256,1,130]{0,2,1:T(8,128)S(1)}, u32[]{:S(2)}, u32[]{:S(2)}) collective-permute-start(f32[256,1,130]{0,2,1:T(8,128)S(1)} %pad_maximum_fusion.1), channel_id=1, source_target_pairs={{32,0},{64,32},{96,64},{128,96},{160,128},{192,160},{224,192},{256... | collective-permute-start | bytes 399368 | tf_op jit(solution)/shard_map/ppermute | solution.py:17
  379.7 1.9 collective-permute-start.26
  386.0 108.6 %all-reduce.4.cloned.1.call-done = f32[2,256,128]{2,1,0:T(8,128)} async-done(((f32[2,256,128]{2,1,0:T(8,128)}), f32[2,256,128]{2,1,0:T(8,128)}) %all-reduce.4.cloned.1.call-update) | async-done | bytes 262160 | tf_op jit(solution)/shard_map/psum | solution.py:153
  (162 shorter events, 53.7 us)
Async XLA Ops:
  7.2 31.0 %copy-start = (f32[3,3,256,256]{3,2,1,0:T(8,128)S(1)}, f32[3,3,256,256]{3,2,1,0:T(8,128)}, u32[]{:S(2)}) copy-start(f32[3,3,256,256]{3,2,1,0:T(8,128)} %param.6) | copy-start | bytes 7077892
  7.2 487.4 %all-reduce.4.cloned.1.call-start = ((), (), s32[]{:S(2)}) async-start(), calls=%async_computation | async-start | bytes 524288 | tf_op jit(solution)/shard_map/psum | solution.py:153
  8.7 19.5 %collective-permute-start = (f32[256,1,1]{2,1,0:T(1,128)S(1)}, f32[256,1,1]{2,1,0:T(1,128)S(1)}, u32[]{:S(2)}, u32[]{:S(2)}) collective-permute-start(f32[256,1,1]{2,1,0:T(1,128)S(1)} %get-tuple-element.70), channel_id=1, source_target_pairs={{0,1},{1,2},{2,3},{3,4},{4,5},{5,6},{6,7},{7,8},{8,9},{9,10},{10,1... | collective-permute-start | bytes 3080 | tf_op jit(solution)/shard_map/ppermute | solution.py:16
  13.1 15.2 %collective-permute-start.1 = (f32[256,1,1]{2,1,0:T(1,128)S(1)}, f32[256,1,1]{2,1,0:T(1,128)S(1)}, u32[]{:S(2)}, u32[]{:S(2)}) collective-permute-start(f32[256,1,1]{2,1,0:T(1,128)S(1)} %get-tuple-element.71), channel_id=1, source_target_pairs={{1,0},{2,1},{3,2},{4,3},{5,4},{6,5},{7,6},{8,7},{9,8},{10,9},{11,1... | collective-permute-start | bytes 3080 | tf_op jit(solution)/shard_map/ppermute | solution.py:17
  26.1 22.5 %collective-permute-start.14 = (f32[2,256,1,128]{1,3,2,0:T(8,128)S(1)}, f32[2,256,1,128]{1,3,2,0:T(8,128)S(1)}, u32[]{:S(2)}, u32[]{:S(2)}) collective-permute-start(f32[2,256,1,128]{1,3,2,0:T(8,128)S(1)} %stack.165), channel_id=1, source_target_pairs={{0,16},{1,17},{2,18},{3,19},{4,20},{5,21},{6,22},{7,23},{8,24},{9,... | collective-permute-start | bytes 786440 | tf_op jit(solution)/shard_map/ppermute | solution.py:23
  30.0 8.6 %collective-permute-start.3 = (f32[256,1,130]{2,1,0:T(1,128)S(1)}, f32[256,1,130]{2,1,0:T(1,128)S(1)}, u32[]{:S(2)}, u32[]{:S(2)}) collective-permute-start(f32[256,1,130]{2,1,0:T(1,128)S(1)} %pad_maximum_fusion), channel_id=1, source_target_pairs={{32,0},{64,32},{96,64},{128,96},{160,128},{192,160},{224,192},{256... | collective-permute-start | bytes 399368 | tf_op jit(solution)/shard_map/ppermute | solution.py:17
  33.2 6.4 %collective-permute-start.2 = (f32[256,1,130]{2,1,0:T(1,128)S(1)}, f32[256,1,130]{2,1,0:T(1,128)S(1)}, u32[]{:S(2)}, u32[]{:S(2)}) collective-permute-start(f32[256,1,130]{2,1,0:T(1,128)S(1)} %pad_maximum_fusion), channel_id=1, source_target_pairs={{0,32},{32,64},{64,96},{96,128},{128,160},{160,192},{192,224},{224... | collective-permute-start | bytes 399368 | tf_op jit(solution)/shard_map/ppermute | solution.py:16
  43.8 11.5 %collective-permute-start.4 = (f32[2,256,1,128]{1,3,2,0:T(8,128)}, f32[2,256,1,128]{1,3,2,0:T(8,128)S(1)}, u32[]{:S(2)}, u32[]{:S(2)}) collective-permute-start(f32[2,256,1,128]{1,3,2,0:T(8,128)} %stack.148), channel_id=1, source_target_pairs={{0,16},{1,17},{2,18},{3,19},{4,20},{5,21},{6,22},{7,23},{8,24},{9,... | collective-permute-start | bytes 786440 | tf_op jit(solution)/shard_map/ppermute | solution.py:23
  55.5 10.9 %copy-start.7 = (f32[1,256,1,128]{1,3,2,0:T(8,128)}, f32[1,256,1,128]{1,3,2,0:T(8,128)S(1)}, u32[]{:S(2)}) copy-start(f32[1,256,1,128]{1,3,2,0:T(8,128)S(1)} %get-tuple-element.31) | copy-start | bytes 393220
  55.5 59.1 %copy-start.3 = (f32[1,256,1,128]{1,3,2,0:T(8,128)}, f32[1,256,1,128]{1,3,2,0:T(8,128)S(1)}, u32[]{:S(2)}) copy-start(f32[1,256,1,128]{1,3,2,0:T(8,128)S(1)} %get-tuple-element.92) | copy-start | bytes 393220
  55.5 59.1 %copy-start.4 = (f32[1,256,1,128]{1,3,2,0:T(8,128)}, f32[1,256,1,128]{1,3,2,0:T(8,128)S(1)}, u32[]{:S(2)}) copy-start(f32[1,256,1,128]{1,3,2,0:T(8,128)S(1)} %get-tuple-element.93) | copy-start | bytes 393220
  56.4 35.1 %collective-permute-start.5 = (f32[2,256,1,128]{1,3,2,0:T(8,128)}, f32[2,256,1,128]{1,3,2,0:T(8,128)}, u32[]{:S(2)}, u32[]{:S(2)}) collective-permute-start(f32[2,256,1,128]{1,3,2,0:T(8,128)} %maximum_select_fusion), channel_id=1, source_target_pairs={{0,8},{1,9},{2,10},{3,11},{4,12},{5,13},{6,14},{7,15},{8,0},{9,1},... | collective-permute-start | bytes 786440 | tf_op jit(solution)/shard_map/ppermute | solution.py:23
  66.4 46.9 %collective-permute-start.15 = (f32[2,256,1,128]{1,3,2,0:T(8,128)}, f32[2,256,1,128]{1,3,2,0:T(8,128)}, u32[]{:S(2)}, u32[]{:S(2)}) collective-permute-start(f32[2,256,1,128]{1,3,2,0:T(8,128)} %maximum_select_fusion.10), channel_id=1, source_target_pairs={{0,8},{1,9},{2,10},{3,11},{4,12},{5,13},{6,14},{7,15},{8,0},{9,1},... | collective-permute-start | bytes 786440 | tf_op jit(solution)/shard_map/ppermute | solution.py:23
  71.2 43.4 %copy-start.6 = (f32[1,256,1,128]{1,3,2,0:T(8,128)S(1)}, f32[1,256,1,128]{1,3,2,0:T(8,128)}, u32[]{:S(2)}) copy-start(f32[1,256,1,128]{1,3,2,0:T(8,128)} %copy-done.5) | copy-start | bytes 393220
  71.2 43.4 %copy-start.8 = (f32[1,256,1,128]{1,3,2,0:T(8,128)S(1)}, f32[1,256,1,128]{1,3,2,0:T(8,128)}, u32[]{:S(2)}) copy-start(f32[1,256,1,128]{1,3,2,0:T(8,128)} %copy-done.7) | copy-start | bytes 393220
  115.6 40.6 %collective-permute-start.16 = (f32[2,256,1,128]{1,3,2,0:T(8,128)S(1)}, f32[2,256,1,128]{1,3,2,0:T(8,128)}, u32[]{:S(2)}, u32[]{:S(2)}) collective-permute-start(f32[2,256,1,128]{1,3,2,0:T(8,128)S(1)} %maximum_select_fusion.11), channel_id=1, source_target_pairs={{0,4},{1,5},{2,6},{3,7},{4,0},{5,1},{6,2},{7,3},{8,12},{9,13},{10,... | collective-permute-start | bytes 786440 | tf_op jit(solution)/shard_map/ppermute | solution.py:23
  118.7 43.2 %collective-permute-start.6 = (f32[2,256,1,128]{1,3,2,0:T(8,128)S(1)}, f32[2,256,1,128]{1,3,2,0:T(8,128)}, u32[]{:S(2)}, u32[]{:S(2)}) collective-permute-start(f32[2,256,1,128]{1,3,2,0:T(8,128)S(1)} %maximum_select_fusion.1), channel_id=1, source_target_pairs={{0,4},{1,5},{2,6},{3,7},{4,0},{5,1},{6,2},{7,3},{8,12},{9,13},{10,... | collective-permute-start | bytes 786440 | tf_op jit(solution)/shard_map/ppermute | solution.py:23
  126.0 40.9 %copy-start.15 = (f32[128]{0:T(128)}, f32[128]{0:T(128)S(1)}, u32[]{:S(2)}) copy-start(f32[128]{0:T(128)S(1)} %get-tuple-element.98) | copy-start | bytes 1540
  126.1 40.9 %copy-start.17 = (f32[128]{0:T(128)}, f32[128]{0:T(128)S(1)}, u32[]{:S(2)}) copy-start(f32[128]{0:T(128)S(1)} %get-tuple-element.99) | copy-start | bytes 1540
  164.0 17.5 %collective-permute-start.17 = (f32[2,256,1,128]{1,3,2,0:T(8,128)S(1)}, f32[2,256,1,128]{1,3,2,0:T(8,128)}, u32[]{:S(2)}, u32[]{:S(2)}) collective-permute-start(f32[2,256,1,128]{1,3,2,0:T(8,128)S(1)} %maximum_select_fusion.12), channel_id=1, source_target_pairs={{0,2},{1,3},{2,0},{3,1},{4,6},{5,7},{6,4},{7,5},{8,10},{9,11},{10,... | collective-permute-start | bytes 786440 | tf_op jit(solution)/shard_map/ppermute | solution.py:23
  167.0 20.2 %collective-permute-start.7 = (f32[2,256,1,128]{1,3,2,0:T(8,128)S(1)}, f32[2,256,1,128]{1,3,2,0:T(8,128)}, u32[]{:S(2)}, u32[]{:S(2)}) collective-permute-start(f32[2,256,1,128]{1,3,2,0:T(8,128)S(1)} %maximum_select_fusion.2), channel_id=1, source_target_pairs={{0,2},{1,3},{2,0},{3,1},{4,6},{5,7},{6,4},{7,5},{8,10},{9,11},{10,... | collective-permute-start | bytes 786440 | tf_op jit(solution)/shard_map/ppermute | solution.py:23
  171.3 20.9 %copy-start.19 = (f32[128]{0:T(128)}, f32[128]{0:T(128)S(1)}, u32[]{:S(2)}) copy-start(f32[128]{0:T(128)S(1)} %get-tuple-element.100) | copy-start | bytes 1540
  171.3 20.9 %copy-start.21 = (f32[128]{0:T(128)}, f32[128]{0:T(128)S(1)}, u32[]{:S(2)}) copy-start(f32[128]{0:T(128)S(1)} %get-tuple-element.101) | copy-start | bytes 1540
  189.3 9.4 %collective-permute-start.18 = (f32[2,256,1,128]{1,3,2,0:T(8,128)S(1)}, f32[2,256,1,128]{1,3,2,0:T(8,128)}, u32[]{:S(2)}, u32[]{:S(2)}) collective-permute-start(f32[2,256,1,128]{1,3,2,0:T(8,128)S(1)} %maximum_select_fusion.13), channel_id=1, source_target_pairs={{0,1},{1,0},{2,3},{3,2},{4,5},{5,4},{6,7},{7,6},{8,9},{9,8},{10,11... | collective-permute-start | bytes 786440 | tf_op jit(solution)/shard_map/ppermute | solution.py:23
  192.2 11.9 %collective-permute-start.8 = (f32[2,256,1,128]{1,3,2,0:T(8,128)S(1)}, f32[2,256,1,128]{1,3,2,0:T(8,128)S(1)}, u32[]{:S(2)}, u32[]{:S(2)}) collective-permute-start(f32[2,256,1,128]{1,3,2,0:T(8,128)S(1)} %maximum_select_fusion.3), channel_id=1, source_target_pairs={{0,1},{1,0},{2,3},{3,2},{4,5},{5,4},{6,7},{7,6},{8,9},{9,8},{10,11... | collective-permute-start | bytes 786440 | tf_op jit(solution)/shard_map/ppermute | solution.py:23
  214.6 14.7 %copy-start.20 = (f32[128]{0:T(128)S(1)}, f32[128]{0:T(128)}, u32[]{:S(2)}) copy-start(f32[128]{0:T(128)} %copy-done.19) | copy-start | bytes 1540
  214.6 14.7 %copy-start.22 = (f32[128]{0:T(128)S(1)}, f32[128]{0:T(128)}, u32[]{:S(2)}) copy-start(f32[128]{0:T(128)} %copy-done.21) | copy-start | bytes 1540
  215.2 8.4 %collective-permute-start.19 = (f32[2,256,1,128]{1,3,2,0:T(8,128)S(1)}, f32[2,256,1,128]{1,3,2,0:T(8,128)S(1)}, u32[]{:S(2)}, u32[]{:S(2)}) collective-permute-start(f32[2,256,1,128]{1,3,2,0:T(8,128)S(1)} %maximum_select_fusion.15), channel_id=1, source_target_pairs={{0,1},{1,0},{2,3},{3,2},{4,5},{5,4},{6,7},{7,6},{8,9},{9,8},{10,11... | collective-permute-start | bytes 786440 | tf_op jit(solution)/shard_map/ppermute | solution.py:23
  217.5 11.7 %collective-permute-start.9 = (f32[2,256,1,128]{1,3,2,0:T(8,128)S(1)}, f32[2,256,1,128]{1,3,2,0:T(8,128)S(1)}, u32[]{:S(2)}, u32[]{:S(2)}) collective-permute-start(f32[2,256,1,128]{1,3,2,0:T(8,128)S(1)} %maximum_select_fusion.5), channel_id=1, source_target_pairs={{0,1},{1,0},{2,3},{3,2},{4,5},{5,4},{6,7},{7,6},{8,9},{9,8},{10,11... | collective-permute-start | bytes 786440 | tf_op jit(solution)/shard_map/ppermute | solution.py:23
  229.3 27.7 %copy-start.16 = (f32[128]{0:T(128)S(1)}, f32[128]{0:T(128)}, u32[]{:S(2)}) copy-start(f32[128]{0:T(128)} %copy-done.15) | copy-start | bytes 1540
  229.3 27.7 %copy-start.18 = (f32[128]{0:T(128)S(1)}, f32[128]{0:T(128)}, u32[]{:S(2)}) copy-start(f32[128]{0:T(128)} %copy-done.17) | copy-start | bytes 1540
  229.5 21.8 %collective-permute-start.10 = (f32[2,256,1,128]{1,3,2,0:T(8,128)S(1)}, f32[2,256,1,128]{1,3,2,0:T(8,128)S(1)}, u32[]{:S(2)}, u32[]{:S(2)}) collective-permute-start(f32[2,256,1,128]{1,3,2,0:T(8,128)S(1)} %maximum_select_fusion.6), channel_id=1, source_target_pairs={{0,2},{1,3},{2,0},{3,1},{4,6},{5,7},{6,4},{7,5},{8,10},{9,11},{10,... | collective-permute-start | bytes 786440 | tf_op jit(solution)/shard_map/ppermute | solution.py:23
  231.5 25.5 %collective-permute-start.20 = (f32[2,256,1,128]{1,3,2,0:T(8,128)S(1)}, f32[2,256,1,128]{1,3,2,0:T(8,128)S(1)}, u32[]{:S(2)}, u32[]{:S(2)}) collective-permute-start(f32[2,256,1,128]{1,3,2,0:T(8,128)S(1)} %maximum_select_fusion.16), channel_id=1, source_target_pairs={{0,2},{1,3},{2,0},{3,1},{4,6},{5,7},{6,4},{7,5},{8,10},{9,11},{10,... | collective-permute-start | bytes 786440 | tf_op jit(solution)/shard_map/ppermute | solution.py:23
  257.2 44.8 %collective-permute-start.11 = (f32[2,256,1,128]{1,3,2,0:T(8,128)S(1)}, f32[2,256,1,128]{1,3,2,0:T(8,128)S(1)}, u32[]{:S(2)}, u32[]{:S(2)}) collective-permute-start(f32[2,256,1,128]{1,3,2,0:T(8,128)S(1)} %maximum_select_fusion.7), channel_id=1, source_target_pairs={{0,4},{1,5},{2,6},{3,7},{4,0},{5,1},{6,2},{7,3},{8,12},{9,13},{10,... | collective-permute-start | bytes 786440 | tf_op jit(solution)/shard_map/ppermute | solution.py:23
  261.1 57.9 %collective-permute-start.21 = (f32[2,256,1,128]{1,3,2,0:T(8,128)S(1)}, f32[2,256,1,128]{1,3,2,0:T(8,128)S(1)}, u32[]{:S(2)}, u32[]{:S(2)}) collective-permute-start(f32[2,256,1,128]{1,3,2,0:T(8,128)S(1)} %maximum_select_fusion.17), channel_id=1, source_target_pairs={{0,4},{1,5},{2,6},{3,7},{4,0},{5,1},{6,2},{7,3},{8,12},{9,13},{10,... | collective-permute-start | bytes 786440 | tf_op jit(solution)/shard_map/ppermute | solution.py:23
  319.2 17.8 %copy-start.9 = (f32[1,256,1,128]{1,3,2,0:T(8,128)}, f32[1,256,1,128]{1,3,2,0:T(8,128)S(1)}, u32[]{:S(2)}) copy-start(f32[1,256,1,128]{1,3,2,0:T(8,128)S(1)} %get-tuple-element.78) | copy-start | bytes 393220
  320.6 21.9 %collective-permute-start.12 = (f32[2,256,1,128]{1,3,2,0:T(8,128)}, f32[2,256,1,128]{1,3,2,0:T(8,128)}, u32[]{:S(2)}, u32[]{:S(2)}) collective-permute-start(f32[2,256,1,128]{1,3,2,0:T(8,128)} %maximum_select_fusion.8), channel_id=1, source_target_pairs={{0,8},{1,9},{2,10},{3,11},{4,12},{5,13},{6,14},{7,15},{8,0},{9,1},... | collective-permute-start | bytes 786440 | tf_op jit(solution)/shard_map/ppermute | solution.py:23
  331.6 18.0 %collective-permute-start.22 = (f32[2,256,1,128]{1,3,2,0:T(8,128)}, f32[2,256,1,128]{1,3,2,0:T(8,128)}, u32[]{:S(2)}, u32[]{:S(2)}) collective-permute-start(f32[2,256,1,128]{1,3,2,0:T(8,128)} %maximum_select_fusion.18), channel_id=1, source_target_pairs={{0,8},{1,9},{2,10},{3,11},{4,12},{5,13},{6,14},{7,15},{8,0},{9,1},... | collective-permute-start | bytes 786440 | tf_op jit(solution)/shard_map/ppermute | solution.py:23
  337.7 15.0 %copy-start.12 = (f32[1,256,128]{2,1,0:T(8,128)S(1)}, f32[1,256,128]{2,1,0:T(8,128)}, u32[]{:S(2)}) copy-start(f32[1,256,128]{2,1,0:T(8,128)} %get-tuple-element.6) | copy-start | bytes 393220
  337.7 15.0 %copy-start.13 = (f32[1,256,128]{2,1,0:T(8,128)S(1)}, f32[1,256,128]{2,1,0:T(8,128)}, u32[]{:S(2)}) copy-start(f32[1,256,128]{2,1,0:T(8,128)} %get-tuple-element.7) | copy-start | bytes 393220
  343.6 28.4 %copy-start.1 = (f32[3,3,256,256]{2,3,1,0:T(8,128)S(1)}, f32[3,3,256,256]{2,3,1,0:T(8,128)}, u32[]{:S(2)}) copy-start(f32[3,3,256,256]{2,3,1,0:T(8,128)} %reverse_bitcast_fusion) | copy-start | bytes 7077892
  350.6 22.6 %copy-start.11 = (f32[256,1,128]{0,2,1:T(8,128)S(1)}, f32[256,1,128]{0,2,1:T(8,128)}, u32[]{:S(2)}) copy-start(f32[256,1,128]{0,2,1:T(8,128)} %copy.12) | copy-start | bytes 393220
  350.8 9.5 %collective-permute-start.23 = (f32[2,256,1,128]{1,3,2,0:T(8,128)S(1)}, f32[2,256,1,128]{1,3,2,0:T(8,128)}, u32[]{:S(2)}, u32[]{:S(2)}) collective-permute-start(f32[2,256,1,128]{1,3,2,0:T(8,128)S(1)} %maximum_select_fusion.19), channel_id=1, source_target_pairs={{0,16},{1,17},{2,18},{3,19},{4,20},{5,21},{6,22},{7,23},{8,24},{9,... | collective-permute-start | bytes 786440 | tf_op jit(solution)/shard_map/ppermute | solution.py:23
  353.5 19.7 %collective-permute-start.13 = (f32[2,256,1,128]{1,3,2,0:T(8,128)S(1)}, f32[2,256,1,128]{1,3,2,0:T(8,128)S(1)}, u32[]{:S(2)}, u32[]{:S(2)}) collective-permute-start(f32[2,256,1,128]{1,3,2,0:T(8,128)S(1)} %maximum_select_fusion.9), channel_id=1, source_target_pairs={{0,16},{1,17},{2,18},{3,19},{4,20},{5,21},{6,22},{7,23},{8,24},{9,... | collective-permute-start | bytes 786440 | tf_op jit(solution)/shard_map/ppermute | solution.py:23
  361.2 12.8 %collective-permute-start.24 = (f32[256,1,1]{0,2,1:T(1,128)S(1)}, f32[256,1,1]{0,2,1:T(1,128)S(1)}, u32[]{:S(2)}, u32[]{:S(2)}) collective-permute-start(f32[256,1,1]{0,2,1:T(1,128)S(1)} %get-tuple-element.62), channel_id=1, source_target_pairs={{0,1},{1,2},{2,3},{3,4},{4,5},{5,6},{6,7},{7,8},{8,9},{9,10},{10,1... | collective-permute-start | bytes 3080 | tf_op jit(solution)/shard_map/ppermute | solution.py:16
  363.1 10.9 %collective-permute-start.25 = (f32[256,1,1]{0,2,1:T(1,128)S(1)}, f32[256,1,1]{0,2,1:T(1,128)S(1)}, u32[]{:S(2)}, u32[]{:S(2)}) collective-permute-start(f32[256,1,1]{0,2,1:T(1,128)S(1)} %get-tuple-element.63), channel_id=1, source_target_pairs={{1,0},{2,1},{3,2},{4,3},{5,4},{6,5},{7,6},{8,7},{9,8},{10,9},{11,1... | collective-permute-start | bytes 3080 | tf_op jit(solution)/shard_map/ppermute | solution.py:17
  374.0 7.9 %collective-permute-start.27 = (f32[256,1,130]{0,2,1:T(8,128)S(1)}, f32[256,1,130]{0,2,1:T(8,128)S(1)}, u32[]{:S(2)}, u32[]{:S(2)}) collective-permute-start(f32[256,1,130]{0,2,1:T(8,128)S(1)} %pad_maximum_fusion.1), channel_id=1, source_target_pairs={{32,0},{64,32},{96,64},{128,96},{160,128},{192,160},{224,192},{256... | collective-permute-start | bytes 399368 | tf_op jit(solution)/shard_map/ppermute | solution.py:17
  379.7 4.0 collective-permute-start.26
  (4 other events, 19.2 us)
Sparse Core Ops, SparseCore 0:
  353.6 140.9 all-reduce.3
where the time goes:
time: 505 us; the launch traced here: 503 us
  waiting for transfers between devices  309 us (61%)
  starting transfers between devices  124 us (25%)
  other arithmetic  27 us (5%)
  matrix products  16.7 us (3%)
  between operations  15.3 us (3%)
  local copies, waits for them, and re-layouts  10.8 us (2%)
    ppermute x20, waiting for transfers between devices, partner(): lax.ppermute(array, axis, [(i, i ^ 1 << stride) for i in range(lax.axis_s...  200 us
    psum x1, waiting for transfers between devices, on_device(): filter_grad = lax.psum(local_grad, 'lat')  109 us
    ppermute x20, starting transfers between devices, partner(): lax.ppermute(array, axis, [(i, i ^ 1 << stride) for i in range(lax.axis_s...  83 us
    ppermute x4, starting transfers between devices, padded_2(): after = lax.ppermute(leading, axis, down)  29.6 us
    ppermute x4, starting transfers between devices, padded_2(): before = lax.ppermute(last, axis, up)  11.3 us
  transfers between devices with their start and end apart: 29, of which 20 were waited for; matrix products, arithmetic and copies ran while one was open for 6% of the time, Pallas kernels for 0%

commit v1 on v0

--- a/solution.py
+++ b/solution.py
@@ -150,7 +150,7 @@
         )
         / total_len
     )
-    filter_grad = lax.psum(local_grad, "lat")
+    filter_grad = lax.all_gather(local_grad, "lat").sum(axis=0)
     flipped_taps = jnp.transpose(conv_weight[::-1, ::-1], (0, 1, 3, 2))
     input_grad = cotangent + apply_taps(with_rims(back_field), flipped_taps, lat_rows, columns)
     return (output, input_grad, filter_grad)

time: 505 us -> 407 us (0.81); the launches traced: 503 us -> 399 us
  waiting for transfers between devices: 309 us -> 209 us
    psum x1 -> x0, waiting for transfers between devices: 109 us -> none  [on_device(): filter_grad = lax.psum(local_grad, 'lat')]
    ppermute x4, waiting for transfers between devices: 1.13 us -> 11.7 us  [padded_2(): before = lax.ppermute(last, axis, up)]
    ppermute x4, starting transfers between devices: 29.6 us -> 23.9 us  [padded_2(): after = lax.ppermute(leading, axis, down)]
  transfers between devices with their start and end apart: 29 -> 29, of which waited for: 20 -> 21; matrix products, arithmetic and copies ran while one was open for 6% -> 8% of each run, Pallas kernels for 0% -> 0%
where the time goes in v1:
time: 407 us; the launch traced here: 399 us
  waiting for transfers between devices  209 us (51%)
  starting transfers between devices  120 us (29%)
  other arithmetic  29.6 us (7%)
  matrix products  16.1 us (4%)
  between operations  15.3 us (4%)
  local copies, waits for them, and re-layouts  9.51 us (2%)
    ppermute x20, waiting for transfers between devices, partner(): lax.ppermute(array, axis, [(i, i ^ 1 << stride) for i in range(lax.axis_s...  197 us
    ppermute x20, starting transfers between devices, partner(): lax.ppermute(array, axis, [(i, i ^ 1 << stride) for i in range(lax.axis_s...  86.5 us
    ppermute x4, starting transfers between devices, padded_2(): after = lax.ppermute(leading, axis, down)  23.9 us
    ppermute x4, waiting for transfers between devices, padded_2(): before = lax.ppermute(last, axis, up)  11.7 us
    ppermute x4, starting transfers between devices, padded_2(): before = lax.ppermute(last, axis, up)  9.17 us
    select_n x10, other arithmetic, forward_pairs(): data = jnp.where(upper, turned, data + other)  8.78 us
  transfers between devices with their start and end apart: 29, of which 21 were waited for; matrix products, arithmetic and copies ran while one was open for 8% of the time, Pallas kernels for 0%

profile of v1, /device:TPU:1, one launch (start us, length us, event | category | flops | bytes accessed | tf_op | source)
XLA Modules:
  0.0 399.2 jit_solution(2013626577380043928)
XLA Ops:
  8.4 5.5 %collective-permute-start.14 = (f32[2,256,1,128]{1,3,2,0:T(8,128)S(1)}, f32[2,256,1,128]{1,3,2,0:T(8,128)S(1)}, u32[]{:S(2)}, u32[]{:S(2)}) collective-permute-start(f32[2,256,1,128]{1,3,2,0:T(8,128)S(1)} %stack.165), channel_id=1, source_target_pairs={{0,16},{1,17},{2,18},{3,19},{4,20},{5,21},{6,22},{7,23},{8,24},{9,... | collective-permute-start | bytes 786440 | tf_op jit(solution)/shard_map/ppermute | solution.py:23
  15.2 11.1 %collective-permute-start.1 = (f32[256,1,1]{2,1,0:T(1,128)S(1)}, f32[256,1,1]{2,1,0:T(1,128)S(1)}, u32[]{:S(2)}, u32[]{:S(2)}) collective-permute-start(f32[256,1,1]{2,1,0:T(1,128)S(1)} %get-tuple-element.74), channel_id=1, source_target_pairs={{1,0},{2,1},{3,2},{4,3},{5,4},{6,5},{7,6},{8,7},{9,8},{10,9},{11,1... | collective-permute-start | bytes 3080 | tf_op jit(solution)/shard_map/ppermute | solution.py:17
  26.3 1.9 collective-permute-start
  28.2 7.4 %collective-permute-done = f32[256,1,1]{2,1,0:T(1,128)S(1)} collective-permute-done((f32[256,1,1]{2,1,0:T(1,128)S(1)}, f32[256,1,1]{2,1,0:T(1,128)S(1)}, u32[]{:S(2)}, u32[]{:S(2)}) %collective-permute-start) | collective-permute-done | bytes 1056 | tf_op jit(solution)/shard_map/ppermute | solution.py:16
  37.4 4.3 %collective-permute-start.3 = (f32[256,1,130]{2,1,0:T(1,128)S(1)}, f32[256,1,130]{2,1,0:T(1,128)S(1)}, u32[]{:S(2)}, u32[]{:S(2)}) collective-permute-start(f32[256,1,130]{2,1,0:T(1,128)S(1)} %pad_maximum_fusion), channel_id=1, source_target_pairs={{32,0},{64,32},{96,64},{128,96},{160,128},{192,160},{224,192},{256... | collective-permute-start | bytes 399368 | tf_op jit(solution)/shard_map/ppermute | solution.py:17
  41.7 3.1 collective-permute-start.2
  52.3 4.6 %collective-permute-start.4 = (f32[2,256,1,128]{1,3,2,0:T(8,128)}, f32[2,256,1,128]{1,3,2,0:T(8,128)S(1)}, u32[]{:S(2)}, u32[]{:S(2)}) collective-permute-start(f32[2,256,1,128]{1,3,2,0:T(8,128)} %stack.148), channel_id=1, source_target_pairs={{0,16},{1,17},{2,18},{3,19},{4,20},{5,21},{6,22},{7,23},{8,24},{9,... | collective-permute-start | bytes 786440 | tf_op jit(solution)/shard_map/ppermute | solution.py:23
  57.1 6.7 %collective-permute-done.4 = f32[2,256,1,128]{1,3,2,0:T(8,128)S(1)} collective-permute-done((f32[2,256,1,128]{1,3,2,0:T(8,128)}, f32[2,256,1,128]{1,3,2,0:T(8,128)S(1)}, u32[]{:S(2)}, u32[]{:S(2)}) %collective-permute-start.4) | collective-permute-done | bytes 262176 | tf_op jit(solution)/shard_map/ppermute | solution.py:23
  65.4 3.7 collective-permute-start.15
  69.9 10.3 %collective-permute-start.5 = (f32[2,256,1,128]{1,3,2,0:T(8,128)}, f32[2,256,1,128]{1,3,2,0:T(8,128)}, u32[]{:S(2)}, u32[]{:S(2)}) collective-permute-start(f32[2,256,1,128]{1,3,2,0:T(8,128)} %maximum_select_fusion), channel_id=1, source_target_pairs={{0,8},{1,9},{2,10},{3,11},{4,12},{5,13},{6,14},{7,15},{8,0},{9,1},... | collective-permute-start | bytes 786440 | tf_op jit(solution)/shard_map/ppermute | solution.py:23
  80.2 35.4 %collective-permute-done.15 = f32[2,256,1,128]{1,3,2,0:T(8,128)} collective-permute-done((f32[2,256,1,128]{1,3,2,0:T(8,128)}, f32[2,256,1,128]{1,3,2,0:T(8,128)}, u32[]{:S(2)}, u32[]{:S(2)}) %collective-permute-start.15) | collective-permute-done | bytes 262176 | tf_op jit(solution)/shard_map/ppermute | solution.py:23
  116.7 4.5 %collective-permute-done.5 = f32[2,256,1,128]{1,3,2,0:T(8,128)} collective-permute-done((f32[2,256,1,128]{1,3,2,0:T(8,128)}, f32[2,256,1,128]{1,3,2,0:T(8,128)}, u32[]{:S(2)}, u32[]{:S(2)}) %collective-permute-start.5) | collective-permute-done | bytes 262176 | tf_op jit(solution)/shard_map/ppermute | solution.py:23
  123.5 1.9 collective-permute-start.16
  126.5 7.3 %collective-permute-start.6 = (f32[2,256,1,128]{1,3,2,0:T(8,128)S(1)}, f32[2,256,1,128]{1,3,2,0:T(8,128)}, u32[]{:S(2)}, u32[]{:S(2)}) collective-permute-start(f32[2,256,1,128]{1,3,2,0:T(8,128)S(1)} %maximum_select_fusion.1), channel_id=1, source_target_pairs={{0,4},{1,5},{2,6},{3,7},{4,0},{5,1},{6,2},{7,3},{8,12},{9,13},{10,... | collective-permute-start | bytes 786440 | tf_op jit(solution)/shard_map/ppermute | solution.py:23
  133.9 22.2 %collective-permute-done.16 = f32[2,256,1,128]{1,3,2,0:T(8,128)} collective-permute-done((f32[2,256,1,128]{1,3,2,0:T(8,128)S(1)}, f32[2,256,1,128]{1,3,2,0:T(8,128)}, u32[]{:S(2)}, u32[]{:S(2)}) %collective-permute-start.16) | collective-permute-done | bytes 262176 | tf_op jit(solution)/shard_map/ppermute | solution.py:23
  157.1 4.6 %collective-permute-done.6 = f32[2,256,1,128]{1,3,2,0:T(8,128)} collective-permute-done((f32[2,256,1,128]{1,3,2,0:T(8,128)S(1)}, f32[2,256,1,128]{1,3,2,0:T(8,128)}, u32[]{:S(2)}, u32[]{:S(2)}) %collective-permute-start.6) | collective-permute-done | bytes 262176 | tf_op jit(solution)/shard_map/ppermute | solution.py:23
  163.8 1.9 collective-permute-start.17
  166.8 4.3 %collective-permute-start.7 = (f32[2,256,1,128]{1,3,2,0:T(8,128)S(1)}, f32[2,256,1,128]{1,3,2,0:T(8,128)S(1)}, u32[]{:S(2)}, u32[]{:S(2)}) collective-permute-start(f32[2,256,1,128]{1,3,2,0:T(8,128)S(1)} %maximum_select_fusion.2), channel_id=1, source_target_pairs={{0,2},{1,3},{2,0},{3,1},{4,6},{5,7},{6,4},{7,5},{8,10},{9,11},{10,... | collective-permute-start | bytes 786440 | tf_op jit(solution)/shard_map/ppermute | solution.py:23
  171.1 11.8 %collective-permute-done.17 = f32[2,256,1,128]{1,3,2,0:T(8,128)} collective-permute-done((f32[2,256,1,128]{1,3,2,0:T(8,128)S(1)}, f32[2,256,1,128]{1,3,2,0:T(8,128)}, u32[]{:S(2)}, u32[]{:S(2)}) %collective-permute-start.17) | collective-permute-done | bytes 262176 | tf_op jit(solution)/shard_map/ppermute | solution.py:23
  183.9 4.5 %collective-permute-done.7 = f32[2,256,1,128]{1,3,2,0:T(8,128)S(1)} collective-permute-done((f32[2,256,1,128]{1,3,2,0:T(8,128)S(1)}, f32[2,256,1,128]{1,3,2,0:T(8,128)S(1)}, u32[]{:S(2)}, u32[]{:S(2)}) %collective-permute-start.7) | collective-permute-done | bytes 262176 | tf_op jit(solution)/shard_map/ppermute | solution.py:23
  190.1 1.9 collective-permute-start.18
  193.1 3.5 collective-permute-start.8
  196.7 2.8 collective-permute-done.18
  200.5 4.5 %collective-permute-done.8 = f32[2,256,1,128]{1,3,2,0:T(8,128)S(1)} collective-permute-done((f32[2,256,1,128]{1,3,2,0:T(8,128)S(1)}, f32[2,256,1,128]{1,3,2,0:T(8,128)S(1)}, u32[]{:S(2)}, u32[]{:S(2)}) %collective-permute-start.8) | collective-permute-done | bytes 262176 | tf_op jit(solution)/shard_map/ppermute | solution.py:23
  216.7 2.2 collective-permute-start.9
  219.7 3.0 collective-permute-start.19
  226.5 4.6 %collective-permute-done.19 = f32[2,256,1,128]{1,3,2,0:T(8,128)} collective-permute-done((f32[2,256,1,128]{1,3,2,0:T(8,128)}, f32[2,256,1,128]{1,3,2,0:T(8,128)}, u32[]{:S(2)}, u32[]{:S(2)}) %collective-permute-start.19) | collective-permute-done | bytes 262176 | tf_op jit(solution)/shard_map/ppermute | solution.py:23
  232.9 1.9 collective-permute-start.10
  234.9 4.3 %collective-permute-start.20 = (f32[2,256,1,128]{1,3,2,0:T(8,128)S(1)}, f32[2,256,1,128]{1,3,2,0:T(8,128)S(1)}, u32[]{:S(2)}, u32[]{:S(2)}) collective-permute-start(f32[2,256,1,128]{1,3,2,0:T(8,128)S(1)} %maximum_select_fusion.16), channel_id=1, source_target_pairs={{0,2},{1,3},{2,0},{3,1},{4,6},{5,7},{6,4},{7,5},{8,10},{9,11},{10,... | collective-permute-start | bytes 786440 | tf_op jit(solution)/shard_map/ppermute | solution.py:23
  239.1 15.6 %collective-permute-done.10 = f32[2,256,1,128]{1,3,2,0:T(8,128)S(1)} collective-permute-done((f32[2,256,1,128]{1,3,2,0:T(8,128)S(1)}, f32[2,256,1,128]{1,3,2,0:T(8,128)S(1)}, u32[]{:S(2)}, u32[]{:S(2)}) %collective-permute-start.10) | collective-permute-done | bytes 262176 | tf_op jit(solution)/shard_map/ppermute | solution.py:23
  254.8 5.6 %collective-permute-done.20 = f32[2,256,1,128]{1,3,2,0:T(8,128)S(1)} collective-permute-done((f32[2,256,1,128]{1,3,2,0:T(8,128)S(1)}, f32[2,256,1,128]{1,3,2,0:T(8,128)S(1)}, u32[]{:S(2)}, u32[]{:S(2)}) %collective-permute-start.20) | collective-permute-done | bytes 262176 | tf_op jit(solution)/shard_map/ppermute | solution.py:23
  260.6 2.1 collective-permute-start.11
  262.8 7.1 %collective-permute-start.21 = (f32[2,256,1,128]{1,3,2,0:T(8,128)S(1)}, f32[2,256,1,128]{1,3,2,0:T(8,128)S(1)}, u32[]{:S(2)}, u32[]{:S(2)}) collective-permute-start(f32[2,256,1,128]{1,3,2,0:T(8,128)S(1)} %maximum_select_fusion.17), channel_id=1, source_target_pairs={{0,4},{1,5},{2,6},{3,7},{4,0},{5,1},{6,2},{7,3},{8,12},{9,13},{10,... | collective-permute-start | bytes 786440 | tf_op jit(solution)/shard_map/ppermute | solution.py:23
  269.9 35.5 %collective-permute-done.11 = f32[2,256,1,128]{1,3,2,0:T(8,128)S(1)} collective-permute-done((f32[2,256,1,128]{1,3,2,0:T(8,128)S(1)}, f32[2,256,1,128]{1,3,2,0:T(8,128)S(1)}, u32[]{:S(2)}, u32[]{:S(2)}) %collective-permute-start.11) | collective-permute-done | bytes 262176 | tf_op jit(solution)/shard_map/ppermute | solution.py:23
  305.4 17.0 %collective-permute-done.21 = f32[2,256,1,128]{1,3,2,0:T(8,128)S(1)} collective-permute-done((f32[2,256,1,128]{1,3,2,0:T(8,128)S(1)}, f32[2,256,1,128]{1,3,2,0:T(8,128)S(1)}, u32[]{:S(2)}, u32[]{:S(2)}) %collective-permute-start.21) | collective-permute-done | bytes 262176 | tf_op jit(solution)/shard_map/ppermute | solution.py:23
  322.6 8.9 %collective-permute-start.12 = (f32[2,256,1,128]{1,3,2,0:T(8,128)S(1)}, f32[2,256,1,128]{1,3,2,0:T(8,128)S(1)}, u32[]{:S(2)}, u32[]{:S(2)}) collective-permute-start(f32[2,256,1,128]{1,3,2,0:T(8,128)S(1)} %maximum_select_fusion.8), channel_id=1, source_target_pairs={{0,8},{1,9},{2,10},{3,11},{4,12},{5,13},{6,14},{7,15},{8,0},{9,1},... | collective-permute-start | bytes 786440 | tf_op jit(solution)/shard_map/ppermute | solution.py:23
  331.5 5.1 %collective-permute-start.22 = (f32[2,256,1,128]{1,3,2,0:T(8,128)S(1)}, f32[2,256,1,128]{1,3,2,0:T(8,128)S(1)}, u32[]{:S(2)}, u32[]{:S(2)}) collective-permute-start(f32[2,256,1,128]{1,3,2,0:T(8,128)S(1)} %maximum_select_fusion.18), channel_id=1, source_target_pairs={{0,8},{1,9},{2,10},{3,11},{4,12},{5,13},{6,14},{7,15},{8,0},{9,1},... | collective-permute-start | bytes 786440 | tf_op jit(solution)/shard_map/ppermute | solution.py:23
  336.7 12.8 %collective-permute-done.12 = f32[2,256,1,128]{1,3,2,0:T(8,128)S(1)} collective-permute-done((f32[2,256,1,128]{1,3,2,0:T(8,128)S(1)}, f32[2,256,1,128]{1,3,2,0:T(8,128)S(1)}, u32[]{:S(2)}, u32[]{:S(2)}) %collective-permute-start.12) | collective-permute-done | bytes 262176 | tf_op jit(solution)/shard_map/ppermute | solution.py:23
  349.5 5.6 %collective-permute-done.22 = f32[2,256,1,128]{1,3,2,0:T(8,128)S(1)} collective-permute-done((f32[2,256,1,128]{1,3,2,0:T(8,128)S(1)}, f32[2,256,1,128]{1,3,2,0:T(8,128)S(1)}, u32[]{:S(2)}, u32[]{:S(2)}) %collective-permute-start.22) | collective-permute-done | bytes 262176 | tf_op jit(solution)/shard_map/ppermute | solution.py:23
  355.3 2.2 collective-permute-start.23
  359.2 4.7 %collective-permute-start.13 = (f32[2,256,1,128]{1,3,2,0:T(8,128)S(1)}, f32[2,256,1,128]{1,3,2,0:T(8,128)S(1)}, u32[]{:S(2)}, u32[]{:S(2)}) collective-permute-start(f32[2,256,1,128]{1,3,2,0:T(8,128)S(1)} %maximum_select_fusion.9), channel_id=1, source_target_pairs={{0,16},{1,17},{2,18},{3,19},{4,20},{5,21},{6,22},{7,23},{8,24},{9,... | collective-permute-start | bytes 786440 | tf_op jit(solution)/shard_map/ppermute | solution.py:23
  363.9 1.9 collective-permute-done.23
  366.8 3.1 collective-permute-start.25
  369.9 2.2 collective-permute-start.24
  374.3 3.6 collective-permute-done.24
  377.8 5.5 %collective-permute-start.27 = (f32[256,1,130]{0,2,1:T(8,128)S(1)}, f32[256,1,130]{0,2,1:T(8,128)S(1)}, u32[]{:S(2)}, u32[]{:S(2)}) collective-permute-start(f32[256,1,130]{0,2,1:T(8,128)S(1)} %pad_maximum_fusion.1), channel_id=1, source_target_pairs={{32,0},{64,32},{96,64},{128,96},{160,128},{192,160},{224,192},{256... | collective-permute-start | bytes 399368 | tf_op jit(solution)/shard_map/ppermute | solution.py:17
  383.4 1.9 collective-permute-start.26
  389.3 3.1 reduce_sum.8
  (152 shorter events, 54.9 us)
Async XLA Ops:
  7.2 39.5 %copy-start = (f32[3,3,256,256]{3,2,1,0:T(8,128)S(1)}, f32[3,3,256,256]{3,2,1,0:T(8,128)}, u32[]{:S(2)}) copy-start(f32[3,3,256,256]{3,2,1,0:T(8,128)} %param.6) | copy-start | bytes 7077892
  7.2 382.1 %all-gather.2.cloned.1.call-start = ((), (), s32[]{:S(2)}) async-start(), calls=%async_computation | async-start | bytes 4456448 | tf_op jit(solution)/shard_map/all_gather | solution.py:153
  8.4 48.7 %collective-permute-start.14 = (f32[2,256,1,128]{1,3,2,0:T(8,128)S(1)}, f32[2,256,1,128]{1,3,2,0:T(8,128)S(1)}, u32[]{:S(2)}, u32[]{:S(2)}) collective-permute-start(f32[2,256,1,128]{1,3,2,0:T(8,128)S(1)} %stack.165), channel_id=1, source_target_pairs={{0,16},{1,17},{2,18},{3,19},{4,20},{5,21},{6,22},{7,23},{8,24},{9,... | collective-permute-start | bytes 786440 | tf_op jit(solution)/shard_map/ppermute | solution.py:23
  15.2 13.0 %collective-permute-start.1 = (f32[256,1,1]{2,1,0:T(1,128)S(1)}, f32[256,1,1]{2,1,0:T(1,128)S(1)}, u32[]{:S(2)}, u32[]{:S(2)}) collective-permute-start(f32[256,1,1]{2,1,0:T(1,128)S(1)} %get-tuple-element.74), channel_id=1, source_target_pairs={{1,0},{2,1},{3,2},{4,3},{5,4},{6,5},{7,6},{8,7},{9,8},{10,9},{11,1... | collective-permute-start | bytes 3080 | tf_op jit(solution)/shard_map/ppermute | solution.py:17
  26.3 9.3 %collective-permute-start = (f32[256,1,1]{2,1,0:T(1,128)S(1)}, f32[256,1,1]{2,1,0:T(1,128)S(1)}, u32[]{:S(2)}, u32[]{:S(2)}) collective-permute-start(f32[256,1,1]{2,1,0:T(1,128)S(1)} %get-tuple-element.73), channel_id=1, source_target_pairs={{0,1},{1,2},{2,3},{3,4},{4,5},{5,6},{6,7},{7,8},{8,9},{9,10},{10,1... | collective-permute-start | bytes 3080 | tf_op jit(solution)/shard_map/ppermute | solution.py:16
  37.4 9.7 %collective-permute-start.3 = (f32[256,1,130]{2,1,0:T(1,128)S(1)}, f32[256,1,130]{2,1,0:T(1,128)S(1)}, u32[]{:S(2)}, u32[]{:S(2)}) collective-permute-start(f32[256,1,130]{2,1,0:T(1,128)S(1)} %pad_maximum_fusion), channel_id=1, source_target_pairs={{32,0},{64,32},{96,64},{128,96},{160,128},{192,160},{224,192},{256... | collective-permute-start | bytes 399368 | tf_op jit(solution)/shard_map/ppermute | solution.py:17
  41.7 6.4 %collective-permute-start.2 = (f32[256,1,130]{2,1,0:T(1,128)S(1)}, f32[256,1,130]{2,1,0:T(1,128)S(1)}, u32[]{:S(2)}, u32[]{:S(2)}) collective-permute-start(f32[256,1,130]{2,1,0:T(1,128)S(1)} %pad_maximum_fusion), channel_id=1, source_target_pairs={{0,32},{32,64},{64,96},{96,128},{128,160},{160,192},{192,224},{224... | collective-permute-start | bytes 399368 | tf_op jit(solution)/shard_map/ppermute | solution.py:16
  46.7 3.3 copy-start.2
  52.3 11.5 %collective-permute-start.4 = (f32[2,256,1,128]{1,3,2,0:T(8,128)}, f32[2,256,1,128]{1,3,2,0:T(8,128)S(1)}, u32[]{:S(2)}, u32[]{:S(2)}) collective-permute-start(f32[2,256,1,128]{1,3,2,0:T(8,128)} %stack.148), channel_id=1, source_target_pairs={{0,16},{1,17},{2,18},{3,19},{4,20},{5,21},{6,22},{7,23},{8,24},{9,... | collective-permute-start | bytes 786440 | tf_op jit(solution)/shard_map/ppermute | solution.py:23
  64.0 0.7 copy-start.5
  64.0 1.4 copy-start.7
  64.0 58.4 %copy-start.3 = (f32[1,256,1,128]{1,3,2,0:T(8,128)}, f32[1,256,1,128]{1,3,2,0:T(8,128)S(1)}, u32[]{:S(2)}) copy-start(f32[1,256,1,128]{1,3,2,0:T(8,128)S(1)} %get-tuple-element.95) | copy-start | bytes 393220
  64.0 58.4 %copy-start.4 = (f32[1,256,1,128]{1,3,2,0:T(8,128)}, f32[1,256,1,128]{1,3,2,0:T(8,128)S(1)}, u32[]{:S(2)}) copy-start(f32[1,256,1,128]{1,3,2,0:T(8,128)S(1)} %get-tuple-element.96) | copy-start | bytes 393220
  65.4 50.2 %collective-permute-start.15 = (f32[2,256,1,128]{1,3,2,0:T(8,128)}, f32[2,256,1,128]{1,3,2,0:T(8,128)}, u32[]{:S(2)}, u32[]{:S(2)}) collective-permute-start(f32[2,256,1,128]{1,3,2,0:T(8,128)} %maximum_select_fusion.10), channel_id=1, source_target_pairs={{0,8},{1,9},{2,10},{3,11},{4,12},{5,13},{6,14},{7,15},{8,0},{9,1},... | collective-permute-start | bytes 786440 | tf_op jit(solution)/shard_map/ppermute | solution.py:23
  69.9 51.4 %collective-permute-start.5 = (f32[2,256,1,128]{1,3,2,0:T(8,128)}, f32[2,256,1,128]{1,3,2,0:T(8,128)}, u32[]{:S(2)}, u32[]{:S(2)}) collective-permute-start(f32[2,256,1,128]{1,3,2,0:T(8,128)} %maximum_select_fusion), channel_id=1, source_target_pairs={{0,8},{1,9},{2,10},{3,11},{4,12},{5,13},{6,14},{7,15},{8,0},{9,1},... | collective-permute-start | bytes 786440 | tf_op jit(solution)/shard_map/ppermute | solution.py:23
  80.2 42.2 %copy-start.6 = (f32[1,256,1,128]{1,3,2,0:T(8,128)S(1)}, f32[1,256,1,128]{1,3,2,0:T(8,128)}, u32[]{:S(2)}) copy-start(f32[1,256,1,128]{1,3,2,0:T(8,128)} %copy-done.5) | copy-start | bytes 393220
  80.2 42.2 %copy-start.8 = (f32[1,256,1,128]{1,3,2,0:T(8,128)S(1)}, f32[1,256,1,128]{1,3,2,0:T(8,128)}, u32[]{:S(2)}) copy-start(f32[1,256,1,128]{1,3,2,0:T(8,128)} %copy-done.7) | copy-start | bytes 393220
  123.5 32.6 %collective-permute-start.16 = (f32[2,256,1,128]{1,3,2,0:T(8,128)S(1)}, f32[2,256,1,128]{1,3,2,0:T(8,128)}, u32[]{:S(2)}, u32[]{:S(2)}) collective-permute-start(f32[2,256,1,128]{1,3,2,0:T(8,128)S(1)} %maximum_select_fusion.11), channel_id=1, source_target_pairs={{0,4},{1,5},{2,6},{3,7},{4,0},{5,1},{6,2},{7,3},{8,12},{9,13},{10,... | collective-permute-start | bytes 786440 | tf_op jit(solution)/shard_map/ppermute | solution.py:23
  126.5 35.2 %collective-permute-start.6 = (f32[2,256,1,128]{1,3,2,0:T(8,128)S(1)}, f32[2,256,1,128]{1,3,2,0:T(8,128)}, u32[]{:S(2)}, u32[]{:S(2)}) collective-permute-start(f32[2,256,1,128]{1,3,2,0:T(8,128)S(1)} %maximum_select_fusion.1), channel_id=1, source_target_pairs={{0,4},{1,5},{2,6},{3,7},{4,0},{5,1},{6,2},{7,3},{8,12},{9,13},{10,... | collective-permute-start | bytes 786440 | tf_op jit(solution)/shard_map/ppermute | solution.py:23
  133.9 32.9 %copy-start.12 = (f32[128]{0:T(128)}, f32[128]{0:T(128)S(1)}, u32[]{:S(2)}) copy-start(f32[128]{0:T(128)S(1)} %get-tuple-element.101) | copy-start | bytes 1540
  133.9 32.9 %copy-start.14 = (f32[128]{0:T(128)}, f32[128]{0:T(128)S(1)}, u32[]{:S(2)}) copy-start(f32[128]{0:T(128)S(1)} %get-tuple-element.102) | copy-start | bytes 1540
  163.8 19.1 %collective-permute-start.17 = (f32[2,256,1,128]{1,3,2,0:T(8,128)S(1)}, f32[2,256,1,128]{1,3,2,0:T(8,128)}, u32[]{:S(2)}, u32[]{:S(2)}) collective-permute-start(f32[2,256,1,128]{1,3,2,0:T(8,128)S(1)} %maximum_select_fusion.12), channel_id=1, source_target_pairs={{0,2},{1,3},{2,0},{3,1},{4,6},{5,7},{6,4},{7,5},{8,10},{9,11},{10,... | collective-permute-start | bytes 786440 | tf_op jit(solution)/shard_map/ppermute | solution.py:23
  166.8 21.6 %collective-permute-start.7 = (f32[2,256,1,128]{1,3,2,0:T(8,128)S(1)}, f32[2,256,1,128]{1,3,2,0:T(8,128)S(1)}, u32[]{:S(2)}, u32[]{:S(2)}) collective-permute-start(f32[2,256,1,128]{1,3,2,0:T(8,128)S(1)} %maximum_select_fusion.2), channel_id=1, source_target_pairs={{0,2},{1,3},{2,0},{3,1},{4,6},{5,7},{6,4},{7,5},{8,10},{9,11},{10,... | collective-permute-start | bytes 786440 | tf_op jit(solution)/shard_map/ppermute | solution.py:23
  171.1 21.9 %copy-start.16 = (f32[128]{0:T(128)}, f32[128]{0:T(128)S(1)}, u32[]{:S(2)}) copy-start(f32[128]{0:T(128)S(1)} %get-tuple-element.103) | copy-start | bytes 1540
  171.1 21.9 %copy-start.17 = (f32[128]{0:T(128)}, f32[128]{0:T(128)S(1)}, u32[]{:S(2)}) copy-start(f32[128]{0:T(128)S(1)} %get-tuple-element.104) | copy-start | bytes 1540
  188.4 0.7 copy-start.10
  190.1 9.4 %collective-permute-start.18 = (f32[2,256,1,128]{1,3,2,0:T(8,128)S(1)}, f32[2,256,1,128]{1,3,2,0:T(8,128)}, u32[]{:S(2)}, u32[]{:S(2)}) collective-permute-start(f32[2,256,1,128]{1,3,2,0:T(8,128)S(1)} %maximum_select_fusion.13), channel_id=1, source_target_pairs={{0,1},{1,0},{2,3},{3,2},{4,5},{5,4},{6,7},{7,6},{8,9},{9,8},{10,11... | collective-permute-start | bytes 786440 | tf_op jit(solution)/shard_map/ppermute | solution.py:23
  193.1 11.9 %collective-permute-start.8 = (f32[2,256,1,128]{1,3,2,0:T(8,128)S(1)}, f32[2,256,1,128]{1,3,2,0:T(8,128)S(1)}, u32[]{:S(2)}, u32[]{:S(2)}) collective-permute-start(f32[2,256,1,128]{1,3,2,0:T(8,128)S(1)} %maximum_select_fusion.3), channel_id=1, source_target_pairs={{0,1},{1,0},{2,3},{3,2},{4,5},{5,4},{6,7},{7,6},{8,9},{9,8},{10,11... | collective-permute-start | bytes 786440 | tf_op jit(solution)/shard_map/ppermute | solution.py:23
  205.2 5.1 %copy-start.11 = (f32[2,256,128]{2,1,0:T(8,128)S(1)}, f32[2,256,128]{2,1,0:T(8,128)}, u32[]{:S(2)}) copy-start(f32[2,256,128]{2,1,0:T(8,128)} %param.7) | copy-start | bytes 786436
  215.3 0.7 copy-start.9
  216.7 8.7 %collective-permute-start.9 = (f32[2,256,1,128]{1,3,2,0:T(8,128)}, f32[2,256,1,128]{1,3,2,0:T(8,128)}, u32[]{:S(2)}, u32[]{:S(2)}) collective-permute-start(f32[2,256,1,128]{1,3,2,0:T(8,128)} %maximum_select_fusion.5), channel_id=1, source_target_pairs={{0,1},{1,0},{2,3},{3,2},{4,5},{5,4},{6,7},{7,6},{8,9},{9,8},{10,11... | collective-permute-start | bytes 786440 | tf_op jit(solution)/shard_map/ppermute | solution.py:23
  219.7 11.3 %collective-permute-start.19 = (f32[2,256,1,128]{1,3,2,0:T(8,128)}, f32[2,256,1,128]{1,3,2,0:T(8,128)}, u32[]{:S(2)}, u32[]{:S(2)}) collective-permute-start(f32[2,256,1,128]{1,3,2,0:T(8,128)} %maximum_select_fusion.15), channel_id=1, source_target_pairs={{0,1},{1,0},{2,3},{3,2},{4,5},{5,4},{6,7},{7,6},{8,9},{9,8},{10,11... | collective-permute-start | bytes 786440 | tf_op jit(solution)/shard_map/ppermute | solution.py:23
  232.0 28.4 %copy-start.13 = (f32[128]{0:T(128)S(1)}, f32[128]{0:T(128)}, u32[]{:S(2)}) copy-start(f32[128]{0:T(128)} %copy-done.12) | copy-start | bytes 1540
  232.0 28.4 %copy-start.15 = (f32[128]{0:T(128)S(1)}, f32[128]{0:T(128)}, u32[]{:S(2)}) copy-start(f32[128]{0:T(128)} %copy-done.14) | copy-start | bytes 1540
  232.9 21.9 %collective-permute-start.10 = (f32[2,256,1,128]{1,3,2,0:T(8,128)S(1)}, f32[2,256,1,128]{1,3,2,0:T(8,128)S(1)}, u32[]{:S(2)}, u32[]{:S(2)}) collective-permute-start(f32[2,256,1,128]{1,3,2,0:T(8,128)S(1)} %maximum_select_fusion.6), channel_id=1, source_target_pairs={{0,2},{1,3},{2,0},{3,1},{4,6},{5,7},{6,4},{7,5},{8,10},{9,11},{10,... | collective-permute-start | bytes 786440 | tf_op jit(solution)/shard_map/ppermute | solution.py:23
  234.9 25.5 %collective-permute-start.20 = (f32[2,256,1,128]{1,3,2,0:T(8,128)S(1)}, f32[2,256,1,128]{1,3,2,0:T(8,128)S(1)}, u32[]{:S(2)}, u32[]{:S(2)}) collective-permute-start(f32[2,256,1,128]{1,3,2,0:T(8,128)S(1)} %maximum_select_fusion.16), channel_id=1, source_target_pairs={{0,2},{1,3},{2,0},{3,1},{4,6},{5,7},{6,4},{7,5},{8,10},{9,11},{10,... | collective-permute-start | bytes 786440 | tf_op jit(solution)/shard_map/ppermute | solution.py:23
  260.6 44.7 %collective-permute-start.11 = (f32[2,256,1,128]{1,3,2,0:T(8,128)S(1)}, f32[2,256,1,128]{1,3,2,0:T(8,128)S(1)}, u32[]{:S(2)}, u32[]{:S(2)}) collective-permute-start(f32[2,256,1,128]{1,3,2,0:T(8,128)S(1)} %maximum_select_fusion.7), channel_id=1, source_target_pairs={{0,4},{1,5},{2,6},{3,7},{4,0},{5,1},{6,2},{7,3},{8,12},{9,13},{10,... | collective-permute-start | bytes 786440 | tf_op jit(solution)/shard_map/ppermute | solution.py:23
  262.8 59.6 %collective-permute-start.21 = (f32[2,256,1,128]{1,3,2,0:T(8,128)S(1)}, f32[2,256,1,128]{1,3,2,0:T(8,128)S(1)}, u32[]{:S(2)}, u32[]{:S(2)}) collective-permute-start(f32[2,256,1,128]{1,3,2,0:T(8,128)S(1)} %maximum_select_fusion.17), channel_id=1, source_target_pairs={{0,4},{1,5},{2,6},{3,7},{4,0},{5,1},{6,2},{7,3},{8,12},{9,13},{10,... | collective-permute-start | bytes 786440 | tf_op jit(solution)/shard_map/ppermute | solution.py:23
  322.6 26.8 %collective-permute-start.12 = (f32[2,256,1,128]{1,3,2,0:T(8,128)S(1)}, f32[2,256,1,128]{1,3,2,0:T(8,128)S(1)}, u32[]{:S(2)}, u32[]{:S(2)}) collective-permute-start(f32[2,256,1,128]{1,3,2,0:T(8,128)S(1)} %maximum_select_fusion.8), channel_id=1, source_target_pairs={{0,8},{1,9},{2,10},{3,11},{4,12},{5,13},{6,14},{7,15},{8,0},{9,1},... | collective-permute-start | bytes 786440 | tf_op jit(solution)/shard_map/ppermute | solution.py:23
  331.5 23.5 %collective-permute-start.22 = (f32[2,256,1,128]{1,3,2,0:T(8,128)S(1)}, f32[2,256,1,128]{1,3,2,0:T(8,128)S(1)}, u32[]{:S(2)}, u32[]{:S(2)}) collective-permute-start(f32[2,256,1,128]{1,3,2,0:T(8,128)S(1)} %maximum_select_fusion.18), channel_id=1, source_target_pairs={{0,8},{1,9},{2,10},{3,11},{4,12},{5,13},{6,14},{7,15},{8,0},{9,1},... | collective-permute-start | bytes 786440 | tf_op jit(solution)/shard_map/ppermute | solution.py:23
  355.3 10.6 %collective-permute-start.23 = (f32[2,256,1,128]{1,3,2,0:T(8,128)S(1)}, f32[2,256,1,128]{1,3,2,0:T(8,128)}, u32[]{:S(2)}, u32[]{:S(2)}) collective-permute-start(f32[2,256,1,128]{1,3,2,0:T(8,128)S(1)} %maximum_select_fusion.19), channel_id=1, source_target_pairs={{0,16},{1,17},{2,18},{3,19},{4,20},{5,21},{6,22},{7,23},{8,24},{9,... | collective-permute-start | bytes 786440 | tf_op jit(solution)/shard_map/ppermute | solution.py:23
  359.1 26.2 %copy-start.1 = (f32[3,3,256,256]{2,3,1,0:T(8,128)S(1)}, f32[3,3,256,256]{2,3,1,0:T(8,128)}, u32[]{:S(2)}) copy-start(f32[3,3,256,256]{2,3,1,0:T(8,128)} %reverse_bitcast_fusion) | copy-start | bytes 7077892
  359.2 14.2 %collective-permute-start.13 = (f32[2,256,1,128]{1,3,2,0:T(8,128)S(1)}, f32[2,256,1,128]{1,3,2,0:T(8,128)S(1)}, u32[]{:S(2)}, u32[]{:S(2)}) collective-permute-start(f32[2,256,1,128]{1,3,2,0:T(8,128)S(1)} %maximum_select_fusion.9), channel_id=1, source_target_pairs={{0,16},{1,17},{2,18},{3,19},{4,20},{5,21},{6,22},{7,23},{8,24},{9,... | collective-permute-start | bytes 786440 | tf_op jit(solution)/shard_map/ppermute | solution.py:23
  366.8 7.4 %collective-permute-start.25 = (f32[256,1,1]{0,2,1:T(1,128)S(1)}, f32[256,1,1]{0,2,1:T(1,128)S(1)}, u32[]{:S(2)}, u32[]{:S(2)}) collective-permute-start(f32[256,1,1]{0,2,1:T(1,128)S(1)} %get-tuple-element.66), channel_id=1, source_target_pairs={{1,0},{2,1},{3,2},{4,3},{5,4},{6,5},{7,6},{8,7},{9,8},{10,9},{11,1... | collective-permute-start | bytes 3080 | tf_op jit(solution)/shard_map/ppermute | solution.py:17
  369.9 7.9 %collective-permute-start.24 = (f32[256,1,1]{0,2,1:T(1,128)S(1)}, f32[256,1,1]{0,2,1:T(1,128)S(1)}, u32[]{:S(2)}, u32[]{:S(2)}) collective-permute-start(f32[256,1,1]{0,2,1:T(1,128)S(1)} %get-tuple-element.65), channel_id=1, source_target_pairs={{0,1},{1,2},{2,3},{3,4},{4,5},{5,6},{6,7},{7,8},{8,9},{9,10},{10,1... | collective-permute-start | bytes 3080 | tf_op jit(solution)/shard_map/ppermute | solution.py:16
  377.8 7.8 %collective-permute-start.27 = (f32[256,1,130]{0,2,1:T(8,128)S(1)}, f32[256,1,130]{0,2,1:T(8,128)S(1)}, u32[]{:S(2)}, u32[]{:S(2)}) collective-permute-start(f32[256,1,130]{0,2,1:T(8,128)S(1)} %pad_maximum_fusion.1), channel_id=1, source_target_pairs={{32,0},{64,32},{96,64},{128,96},{160,128},{192,160},{224,192},{256... | collective-permute-start | bytes 399368 | tf_op jit(solution)/shard_map/ppermute | solution.py:17
  383.4 3.9 collective-permute-start.26
Sparse Core Ops, SparseCore 0:
  223.6 41.9 all-gather.1
